TPU v7x, 32 devices: a whole 2x2x4 slice. The times are simulated.
32 devices in a mesh: pair: 8 (over y, x, core), grp: 4 (over z).
Axes of the slice: x: 2, y: 2, z: 4, core: 2. Of those that a mesh axis runs over, the one named last changes fastest.
Arguments:
- sector_rows: int32 [4], replicated, may hold values from 1 to 256, 768 in all
- wavefunction: bfloat16 [4, 256, 512], P('grp'), may hold values from -6 to 6
- left_ops: bfloat16 [64, 4, 256, 256], P(('pair', 'grp')), may hold values from -0.375 to 0.375
- right_diag: bfloat16 [64, 4, 512], P('pair', 'grp'), may hold values from -0.0078125 to 0.0078125
Outputs:
- slab: float32 [64, 64], P(('pair', 'grp'))
Inputs may be any that keep to these rules, and one draw needn't show every extreme that they name: `sector_rows`: each entry counts the live leading rows of one sector block; at least one sector has 256.
All inputs are finite; a program needn't handle non-finite values.
Results may differ from a plain program's by a relative error of at most 0.0029.
Values may be sent and summed in bfloat16 or wider, within the bound.
No kernel may reach another device: no remote copies, remote signals or barrier semaphores. Data moves between devices by JAX's collectives and lax.ppermute only.
A program may use at most 64 MiB of HBM per device.

v0:
```python
import jax
import jax.numpy as jnp
from jax import lax
from jax.sharding import PartitionSpec as P


def live_states(sector_rows, wavefunction):
    row_index = lax.broadcasted_iota(jnp.int32, wavefunction.shape, 1)
    return jnp.where(
        row_index < sector_rows[:, None, None], wavefunction, jnp.zeros_like(wavefunction)
    )


def local(sector_rows, wavefunction, left_ops, right_diag):
    owned = wavefunction.shape[0]
    first = lax.axis_index("grp") * owned
    right_local = lax.all_gather(right_diag, "pair", axis=0, tiled=True)
    own_rows = lax.dynamic_slice_in_dim(sector_rows, first, owned, 0)
    live = live_states(own_rows, wavefunction)
    blocks = lax.all_to_all(left_ops, "grp", split_axis=1, concat_axis=0, tiled=True)

    def per_pair(block):
        image = jnp.einsum("sab,sbc->sac", block, live, preferred_element_type=jnp.float32)
        return jnp.sum(live.astype(jnp.float32) * image, axis=1)

    weights = lax.map(per_pair, blocks).astype(jnp.bfloat16)
    group_pairs = weights.shape[0]
    flat = weights.reshape(group_pairs, -1)
    diag_flat = right_local.reshape(right_local.shape[0], -1)
    partial_slab = lax.dot_general(
        flat, diag_flat, (((1,), (1,)), ((), ())), preferred_element_type=jnp.float32
    )
    result = lax.psum_scatter(partial_slab, "grp", scatter_dimension=0, tiled=True)
    return result


def solution(mesh):
    in_specs = (
        P(),
        P("grp", None, None),
        P(("pair", "grp"), None, None, None),
        P("pair", "grp", None),
    )
    out_specs = P(("pair", "grp"), None)
    return jax.shard_map(local, mesh=mesh, in_specs=in_specs, out_specs=out_specs, check_vma=False)
```

profile of v0, /device:TPU:0, one launch (start us, length us, event | category | flops | bytes accessed | tf_op | source)
XLA Modules:
  0.0 47.5 jit_solution(5526043052721479483)
XLA Ops:
  0.0 2.3 %copy.8 = bf16[2,4,256,256]{3,2,0,1:T(8,128)(2,1)} copy(bf16[2,4,256,256]{3,2,1,0:T(8,128)(2,1)} %param.8) | data formatting | bytes 2097152 | tf_op args[2]
  2.3 0.0 copy-start.3
  2.3 0.0 copy-start
  2.3 6.5 %all-to-all-start = ((bf16[2,4,256,256]{3,2,0,1:T(8,128)(2,1)}), bf16[2,4,256,256]{3,2,0,1:T(8,128)(2,1)S(1)}, u32[]{:S(2)}, u32[]{:S(2)}) async-start(bf16[2,4,256,256]{3,2,0,1:T(8,128)(2,1)} %copy.8), calls=%async_computation | async-start | bytes 2097152 | tf_op jit(solution)/shard_map/all_to_all | solution.py:20
  8.8 0.0 copy-start.2
  8.8 0.7 %copy-done.2 = s32[4]{0:T(128)S(1)} copy-done((s32[4]{0:T(128)S(1)}, s32[4]{0:T(128)}, u32[]{:S(2)}) %copy-start.2) | copy-done | bytes 40
  9.4 0.6 %dynamic_slice.7 = s32[1]{0:T(128)} dynamic-slice(s32[4]{0:T(128)S(1)} %copy-done.2, s32[]{:T(128)S(6)} %select_n.7), dynamic_slice_sizes={1} | dynamic-slice | bytes 12 | tf_op jit(solution)/shard_map/dynamic_slice | solution.py:18
  10.0 0.0 copy-start.1
  10.0 0.0 copy-done.3
  10.0 0.6 %dynamic-slice = u32[1]{0:T(128)} dynamic-slice(u32[32]{0:T(128)S(1)} %copy-done.3, u32[]{:T(128)S(6)} %add.10), dynamic_slice_sizes={1} | dynamic-slice | bytes 12
  11.3 0.0 copy-done.1
  11.3 9.3 %all_gather.3 = bf16[64,1,512]{2,0,1:T(8,128)(2,1)S(1)} all-gather(bf16[8,1,512]{2,0,1:T(8,128)(2,1)S(1)} %copy-done.1), channel_id=1, replica_groups=mesh['pair'=8,'grp'=4] {'pair'}, dimensions={0}, use_global_device_ids=true | all-gather | bytes 73728 | tf_op jit(solution)/shard_map/all_gather | solution.py:17
  20.6 0.0 copy-done
  20.6 0.7 %fusion.5 = bf16[1,256,512]{2,1,0:T(8,128)(2,1)S(1)} fusion(bf16[1,256,512]{2,1,0:T(8,128)(2,1)S(1)} %copy-done, s32[]{:T(128)} %bitcast.3), kind=kLoop, calls=%fused_computation.7 | loop fusion | flops 262144 | bytes 524292 | tf_op jit(solution)/shard_map/jit(_where)/select_n | solution.py:9
  21.3 13.2 %all-to-all-done = bf16[2,4,256,256]{3,2,0,1:T(8,128)(2,1)S(1)} async-done(((bf16[2,4,256,256]{3,2,0,1:T(8,128)(2,1)}), bf16[2,4,256,256]{3,2,0,1:T(8,128)(2,1)S(1)}, u32[]{:S(2)}, u32[]{:S(2)}) %all-to-all-start) | async-done | bytes 1048608 | tf_op jit(solution)/shard_map/all_to_all | solution.py:20
  34.5 2.5 %while.10 = (s32[]{:T(128)}, bf16[8,1,512]{2,0,1:T(8,128)(2,1)S(1)}, bf16[1,256,512]{2,1,0:T(8,128)(2,1)S(1)}, bf16[8,1,256,256]{3,2,1,0:T(8,128)(2,1)S(1)}, s32[]{:T(128)}, /*index=5*/s32[]{:T(128)}) while((s32[]{:T(128)}, bf16[8,1,512]{2,0,1:T(8,128)(2,1)S(1)}, bf16[1,256,512]{2,1,0:T(8,128)(2,1)S(1)}, ...), condition=%wide.region_2.3_spmd, body=%wide.region_0.2_spmd.sunk | while | flops 67501568 | bytes 661581 | solution.py:26
  34.5 0.2 fusion.15
  34.8 0.2 fusion.15
  35.1 0.2 fusion.15
  35.4 0.2 fusion.15
  35.7 0.2 fusion.15
  36.0 0.2 fusion.15
  36.3 0.2 fusion.15
  36.7 0.2 fusion.15
  37.0 0.1 fusion.6
  37.1 9.8 %all-reduce = f32[8,64]{1,0:T(8,128)S(1)} all-reduce(f32[8,64]{1,0:T(8,128)S(1)} %fusion.6), channel_id=2, replica_groups=mesh['pair'=8,'grp'=4] {'grp'}, use_global_device_ids=true, to_apply=%region_3.4.clone | all-reduce | flops 512 | bytes 4096
  46.9 0.6 %constant_dynamic-slice_fusion = f32[2,64]{1,0:T(2,128)} fusion(f32[8,64]{1,0:T(8,128)S(1)} %all-reduce, u32[]{:T(128)S(6)} %multiply.1), kind=kLoop, calls=%fused_computation.12 | loop fusion | bytes 1028
  (9 shorter events, 0.3 us)
Async XLA Ops:
  2.3 7.8 %copy-start.3 = (u32[32]{0:T(128)S(1)}, u32[32]{0:T(128)}, u32[]{:S(2)}) copy-start(u32[32]{0:T(128)} %constant.28) | copy-start | bytes 388
  2.3 18.3 %copy-start = (bf16[1,256,512]{2,1,0:T(8,128)(2,1)S(1)}, bf16[1,256,512]{2,1,0:T(8,128)(2,1)}, u32[]{:S(2)}) copy-start(bf16[1,256,512]{2,1,0:T(8,128)(2,1)} %param.7) | copy-start | bytes 786436
  2.3 32.2 %all-to-all-start = ((bf16[2,4,256,256]{3,2,0,1:T(8,128)(2,1)}), bf16[2,4,256,256]{3,2,0,1:T(8,128)(2,1)S(1)}, u32[]{:S(2)}, u32[]{:S(2)}) async-start(bf16[2,4,256,256]{3,2,0,1:T(8,128)(2,1)} %copy.8), calls=%async_computation | async-start | bytes 2097152 | tf_op jit(solution)/shard_map/all_to_all | solution.py:20
  8.8 0.7 %copy-start.2 = (s32[4]{0:T(128)S(1)}, s32[4]{0:T(128)}, u32[]{:S(2)}) copy-start(s32[4]{0:T(128)} %param.6) | copy-start | bytes 52
  10.0 1.3 %copy-start.1 = (bf16[8,1,512]{2,0,1:T(8,128)(2,1)S(1)}, bf16[8,1,512]{2,0,1:T(8,128)(2,1)}, u32[]{:S(2)}) copy-start(bf16[8,1,512]{2,0,1:T(8,128)(2,1)} %param.9) | copy-start | bytes 24580
where the time goes:
time: 47.7 us; the launch traced here: 47.5 us
  blocking collectives  19.1 us (40%)
  waiting for transfers between devices  13.2 us (28%)
  starting transfers between devices  6.48 us (14%)
  local copies, waits for them, and re-layouts  5.1 us (11%)
  matrix products  2.07 us (4%)
  other arithmetic  0.7 us (1%)
  between operations  0.67 us (1%)
    all_to_all x1, waiting for transfers between devices, local(): lax.all_to_all(left_ops, 'grp', split_axis=1, concat_axis=0, tiled=True)  13.2 us
    unnamed x1, blocking collectives  9.81 us
    all_gather x1, blocking collectives, local(): right_local = lax.all_gather(right_diag, 'pair', axis=0, tiled=True)  9.26 us
    all_to_all x1, starting transfers between devices, local(): lax.all_to_all(left_ops, 'grp', split_axis=1, concat_axis=0, tiled=True)  6.48 us
    unnamed x11, local copies, waits for them, and re-layouts  4.15 us
    dot_general x8, matrix products, per_pair(): jnp.einsum('sab,sbc->sac', block, live, preferred_element_type=jnp.float32)  1.95 us
  transfers between devices with their start and end apart: 1, of which 1 were waited for; matrix products, arithmetic and copies ran while one was open for 4% of the time, Pallas kernels for 0%

commit v1 on v0

v1 whole, which is shorter than its diff:
```python
import functools

import jax
import jax.numpy as jnp
from jax import lax
from jax.experimental import pallas as pl
from jax.experimental.pallas import tpu as pltpu
from jax.sharding import PartitionSpec as P

LANES = 128
CORES = 2
BOTH = ("pair", "grp")


class Plan:
    def __init__(self, pairs, groups, wave, diag, ops):
        self.pairs, self.groups = pairs, groups
        self.chips = pairs // CORES
        self.rows, self.cols = wave.shape[1], wave.shape[2]
        self.tiles = self.cols // LANES
        self.col_cuts = min(self.chips, self.tiles)
        self.row_cuts = self.chips // self.col_cuts
        self.width = self.cols // self.col_cuts
        self.wide = self.width // LANES
        self.half = self.rows // CORES
        self.piece = self.half // self.row_cuts
        self.diag_rows = diag.shape[0]
        self.live_rows = self.piece * self.wide
        self.tail = self.diag_rows * self.tiles
        self.message = self.live_rows + self.tail
        self.own_pairs = ops.shape[0]

    def batches(self):
        steps = [d for d in range(1, self.groups)]
        near = [d for d in steps if d in (1, self.groups - 1)]
        far = [d for d in steps if d not in near]
        return [b for b in (near, far) if b]


def cut_kernel(plan, rows_ref, wave_ref, diag_ref, out_ref, held, sem):
    me, grp = lax.axis_index("pair"), lax.axis_index("grp")
    core, chip = lax.rem(me, CORES), lax.div(me, CORES)
    col, row = lax.rem(chip, plan.col_cuts), lax.div(chip, plan.col_cuts)
    first = core * plan.half + row * plan.piece
    copy = pltpu.make_async_copy(
        wave_ref.at[
            0,
            pl.ds(pl.multiple_of(first, plan.piece), plan.piece),
            pl.ds(pl.multiple_of(col * plan.width, LANES), plan.width),
        ],
        held,
        sem,
    )
    copy.start()
    diag = diag_ref[:, 0, :]
    for k in range(plan.tiles):
        at = plan.live_rows + k * plan.diag_rows
        out_ref[at : at + plan.diag_rows, :] = diag[:, k * LANES : (k + 1) * LANES]
    limit = rows_ref[grp] - first
    copy.wait()
    index = lax.broadcasted_iota(jnp.int32, held.shape, 0)
    live = jnp.where(index < limit, held[...].astype(jnp.float32), 0.0).astype(jnp.bfloat16)
    for k in range(plan.wide):
        out_ref[k * plan.piece : (k + 1) * plan.piece, :] = live[:, k * LANES : (k + 1) * LANES]


def cut(plan, sector_rows, wave, diag):
    return pl.pallas_call(
        functools.partial(cut_kernel, plan),
        out_shape=jax.ShapeDtypeStruct((plan.message, LANES), jnp.bfloat16),
        in_specs=[
            pl.BlockSpec(memory_space=pltpu.SMEM),
            pl.BlockSpec(memory_space=pl.ANY),
            pl.BlockSpec(memory_space=pltpu.VMEM),
        ],
        out_specs=pl.BlockSpec(memory_space=pltpu.VMEM),
        scratch_shapes=[
            pltpu.VMEM((plan.piece, plan.width), jnp.bfloat16),
            pltpu.SemaphoreType.DMA,
        ],
        name="cut",
    )(sector_rows, wave, diag)


def slab_kernel(plan, batches, rows_ref, wave_ref, ops_ref, *refs):
    count = len(batches)
    mine, theirs = refs[:count], refs[count : 2 * count]
    out_ref, state, diag, weight = refs[2 * count :]
    me, grp = lax.axis_index("pair"), lax.axis_index("grp")
    core, chip = lax.rem(me, CORES), lax.div(me, CORES)
    cols, dr = plan.cols, plan.diag_rows

    weight[...] = jnp.zeros_like(weight)

    def weigh(slot, sector, live):
        wide = live.astype(jnp.float32)
        for p in range(plan.own_pairs):
            image = jnp.dot(ops_ref[p, sector], live, preferred_element_type=jnp.float32)
            total = jnp.sum(wide * image, axis=0, keepdims=True)
            weight[p : p + 1, slot * cols : (slot + 1) * cols] = total

    index = lax.broadcasted_iota(jnp.int32, wave_ref.shape[1:], 0)
    own = jnp.where(index < rows_ref[grp], wave_ref[0].astype(jnp.float32), 0.0)
    weigh(0, grp, own.astype(jnp.bfloat16))

    def place_diag(slot, chip_slot, a, b, at):
        for flip, block in ((0, a), (1, b)):
            q = (chip_slot * CORES + flip) * dr
            for k in range(plan.tiles):
                diag[q : q + dr, slot * cols + k * LANES : slot * cols + (k + 1) * LANES] = (
                    block[chip_slot, at + k * dr : at + (k + 1) * dr, :].astype(jnp.float32)
                )

    slot = 0
    for b, steps in enumerate(batches):
        if b == 0:
            for j in range(plan.chips):
                place_diag(0, j, mine[b], theirs[b], len(steps) * plan.message)
        for t, step in enumerate(steps):
            slot += 1
            at = t * plan.message
            for j in range(plan.chips):
                source = lax.bitwise_xor(chip, j)
                col, row = lax.rem(source, plan.col_cuts), lax.div(source, plan.col_cuts)
                for k in range(plan.wide):
                    a = mine[b][j, at + k * plan.piece : at + (k + 1) * plan.piece, :]
                    o = theirs[b][j, at + k * plan.piece : at + (k + 1) * plan.piece, :]
                    lane = pl.multiple_of(col * plan.width + k * LANES, LANES)
                    mine_at = pl.multiple_of(core * plan.half + row * plan.piece, plan.piece)
                    their_at = pl.multiple_of((1 - core) * plan.half + row * plan.piece, plan.piece)
                    state[pl.ds(mine_at, plan.piece), pl.ds(lane, LANES)] = a
                    state[pl.ds(their_at, plan.piece), pl.ds(lane, LANES)] = o
                place_diag(slot, j, mine[b], theirs[b], at + plan.live_rows)
            sector = lax.rem(grp + plan.groups - step, plan.groups)
            weigh(slot, sector, state[...])

    slab = lax.dot_general(
        weight[...].astype(jnp.bfloat16),
        diag[...].astype(jnp.bfloat16),
        (((1,), (1,)), ((), ())),
        preferred_element_type=jnp.float32,
    )
    total = slab.shape[1]
    lane = lax.broadcasted_iota(jnp.int32, slab.shape, 1)
    bit = 1
    while bit < plan.pairs:
        span = bit * dr
        up = jnp.concatenate([slab[:, span:], slab[:, :span]], axis=1)
        down = jnp.concatenate([slab[:, total - span :], slab[:, : total - span]], axis=1)
        swapped = jnp.where(lax.rem(lax.div(lane, span), 2) == 0, up, down)
        keep = lax.rem(lax.div(me, bit), 2) == 0
        slab = jnp.where(keep, slab, swapped)
        bit *= 2
    out_ref[...] = slab[: plan.own_pairs, :]


def slab_call(plan, batches, sector_rows, wave, ops, mine, theirs):
    total_q = plan.pairs * plan.diag_rows
    vmem = pl.BlockSpec(memory_space=pltpu.VMEM)
    return pl.pallas_call(
        functools.partial(slab_kernel, plan, batches),
        out_shape=jax.ShapeDtypeStruct((plan.own_pairs, total_q), jnp.float32),
        in_specs=[pl.BlockSpec(memory_space=pltpu.SMEM)] + [vmem] * (2 + 2 * len(batches)),
        out_specs=vmem,
        scratch_shapes=[
            pltpu.VMEM((plan.rows, plan.cols), jnp.bfloat16),
            pltpu.VMEM((total_q, plan.groups * plan.cols), jnp.float32),
            pltpu.VMEM((8, plan.groups * plan.cols), jnp.float32),
        ],
        name="slab",
    )(sector_rows, wave, ops, *mine, *theirs)


def local(mesh, sector_rows, wavefunction, left_ops, right_diag):
    pairs, groups = mesh.shape["pair"], mesh.shape["grp"]
    plan = Plan(pairs, groups, wavefunction, right_diag, left_ops)
    batches = plan.batches()

    def send(x, to):
        hops = []
        for p in range(pairs):
            for g in range(groups):
                q, h = to(p, g)
                hops.append((p * groups + g, q * groups + h))
        return lax.ppermute(x, BOTH, hops)

    own = cut(plan, sector_rows, wavefunction, right_diag)
    moved = {}
    for d in [d for steps in batches for d in steps]:
        moved[d] = send(own, lambda p, g: (p, (g + d) % groups))
    mine, theirs = [], []
    for b, steps in enumerate(batches):
        parts = [moved[d] for d in steps]
        if b == 0:
            parts.append(own[plan.live_rows :])
        packed = jnp.concatenate(parts, axis=0) if len(parts) > 1 else parts[0]
        got = [packed]
        for j in range(1, plan.chips):
            got.append(send(packed, lambda p, g: (p ^ (j * CORES), g)))
        stacked = jnp.stack(got)
        mine.append(stacked)
        theirs.append(send(stacked, lambda p, g: (p ^ 1, g)))
    return slab_call(plan, batches, sector_rows, wavefunction, left_ops, mine, theirs)


def solution(mesh):
    in_specs = (
        P(),
        P("grp", None, None),
        P(("pair", "grp"), None, None, None),
        P("pair", "grp", None),
    )
    out_specs = P(("pair", "grp"), None)
    return jax.shard_map(
        functools.partial(local, mesh), mesh=mesh, in_specs=in_specs, out_specs=out_specs, check_vma=False
    )
```

time: 47.7 us -> 36.7 us (0.77)
  blocking collectives: 19.1 us -> 0 us
  starting transfers between devices: 6.48 us -> 12.4 us
  Pallas kernels: 0 us -> 5.52 us
  matrix products: 2.07 us -> 0 us
  local copies, waits for them, and re-layouts: 5.1 us -> 3.47 us
  waiting for transfers between devices: 13.2 us -> 14.8 us
  other arithmetic: 0.7 us -> 0.08 us
  between operations: 0.67 us -> 0.08 us
    ppermute x0 -> x11, waiting for transfers between devices: none -> 14.8 us  [send(): return lax.ppermute(x, BOTH, hops)]
    all_to_all x1 -> x0, waiting for transfers between devices: 13.2 us -> none  [local(): lax.all_to_all(left_ops, 'grp', split_axis=1, concat_axis=0, tiled=True)]
    ppermute x0 -> x11, starting transfers between devices: none -> 12.4 us  [send(): return lax.ppermute(x, BOTH, hops)]
    unnamed x1 -> x0, blocking collectives: 9.81 us -> none
    all_gather x1 -> x0, blocking collectives: 9.26 us -> none  [local(): right_local = lax.all_gather(right_diag, 'pair', axis=0, tiled=True)]
    all_to_all x1 -> x0, starting transfers between devices: 6.48 us -> none  [local(): lax.all_to_all(left_ops, 'grp', split_axis=1, concat_axis=0, tiled=True)]
    pallas_call x0 -> x2, Pallas kernels: none -> 5.52 us  [the longest x1 3.39 us: slab_call(): pl.pallas_call(functools.partial(slab_kernel, plan, batches), out_shape=j...]
    dot_general x9 -> x0, matrix products: 2.07 us -> none  [the longest x8 1.95 us: per_pair(): jnp.einsum('sab,sbc->sac', block, live, preferred_element_type=jnp.float32)]
  transfers between devices with their start and end apart: 1 -> 11, of which waited for: 1 -> 9; matrix products, arithmetic and copies ran while one was open for 4% -> 2% of each run, Pallas kernels for 0% -> 0%
where the time goes in v1:
time: 36.7 us; the launch traced here: 36.3 us
  waiting for transfers between devices  14.8 us (40%)
  starting transfers between devices  12.4 us (34%)
  Pallas kernels  5.52 us (15%)
  local copies, waits for them, and re-layouts  3.47 us (9%)
    ppermute x11, waiting for transfers between devices, send(): return lax.ppermute(x, BOTH, hops)  14.8 us
    ppermute x11, starting transfers between devices, send(): return lax.ppermute(x, BOTH, hops)  12.4 us
    pallas_call x1, Pallas kernels, slab_call(): pl.pallas_call(functools.partial(slab_kernel, plan, batches), out_shape=j...  3.39 us
    unnamed x11, local copies, waits for them, and re-layouts  2.7 us
    pallas_call x1, Pallas kernels, cut(): pl.pallas_call(functools.partial(cut_kernel, plan), out_shape=jax.ShapeDt...  2.12 us
    slice x1, local copies, waits for them, and re-layouts, local(): parts.append(own[plan.live_rows:])  0.76 us
  transfers between devices with their start and end apart: 11, of which 9 were waited for; matrix products, arithmetic and copies ran while one was open for 2% of the time, Pallas kernels for 0%

profile of v1, /device:TPU:0, one launch (start us, length us, event | category | flops | bytes accessed | tf_op | source)
XLA Modules:
  0.0 36.3 jit_solution(13595120392046073501)
XLA Ops:
  0.0 1.3 %copy.5.diag_ref = bf16[8,1,512]{2,1,0:T(2,128)(2,1)} copy(bf16[8,1,512]{2,0,1:T(8,128)(2,1)} %param.7) | data formatting | bytes 16384 | tf_op args[3]
  1.3 2.1 %cut.1 = bf16[160,128]{1,0:T(8,128)(2,1)} custom-call(s32[4]{0:T(128)} %rows_ref.3, bf16[1,256,512]{2,1,0:T(8,128)(2,1)} %wave_ref.3, bf16[8,1,512]{2,1,0:T(2,128)(2,1)} %copy.5.diag_ref), custom_call_target="tpu_custom_call" | custom-call | tf_op jit(solution)/shard_map/cut/pallas_call | solution.py:68
  3.4 5.1 %collective-permute-start.1 = (bf16[160,128]{1,0:T(8,128)(2,1)}, bf16[160,128]{1,0:T(8,128)(2,1)S(1)}, u32[]{:S(2)}, u32[]{:S(2)}) collective-permute-start(bf16[160,128]{1,0:T(8,128)(2,1)} %cut.1), channel_id=1, source_target_pairs={{0,3},{1,0},{2,1},{3,2},{4,7},{5,4},{6,5},{7,6},{8,11},{9,8},{10,9... | collective-permute-start | bytes 122888 | tf_op jit(solution)/shard_map/ppermute | solution.py:185
  8.6 0.0 collective-permute-start
  8.6 0.8 %slice.4 = bf16[32,128]{1,0:T(8,128)(2,1)S(1)} slice(bf16[160,128]{1,0:T(8,128)(2,1)} %cut.1), slice={[128:160], [0:128]} | slice | bytes 16384 | tf_op jit(solution)/shard_map/slice | solution.py:195
  9.3 0.0 copy-start.4
  9.3 1.2 %collective-permute-done.1 = bf16[160,128]{1,0:T(8,128)(2,1)S(1)} collective-permute-done((bf16[160,128]{1,0:T(8,128)(2,1)}, bf16[160,128]{1,0:T(8,128)(2,1)S(1)}, u32[]{:S(2)}, u32[]{:S(2)}) %collective-permute-start.1) | collective-permute-done | bytes 40992 | tf_op jit(solution)/shard_map/ppermute | solution.py:185
  10.6 4.0 %collective-permute-done = bf16[160,128]{1,0:T(8,128)(2,1)S(1)} collective-permute-done((bf16[160,128]{1,0:T(8,128)(2,1)}, bf16[160,128]{1,0:T(8,128)(2,1)S(1)}, u32[]{:S(2)}, u32[]{:S(2)}) %collective-permute-start) | collective-permute-done | bytes 40992 | tf_op jit(solution)/shard_map/ppermute | solution.py:185
  14.6 1.6 %collective-permute-start.3 = (bf16[352,128]{1,0:T(8,128)(2,1)S(1)}, bf16[352,128]{1,0:T(8,128)(2,1)S(1)}, u32[]{:S(2)}, u32[]{:S(2)}) collective-permute-start(bf16[352,128]{1,0:T(8,128)(2,1)S(1)} %get-tuple-element.6), channel_id=1, source_target_pairs={{0,16},{1,17},{2,18},{3,19},{4,20},{5,21},{6,22},{7,23},{8,24},{9,... | collective-permute-start | bytes 270344 | tf_op jit(solution)/shard_map/ppermute | solution.py:185
  16.2 1.5 %collective-permute-start.2 = (bf16[352,128]{1,0:T(8,128)(2,1)S(1)}, bf16[352,128]{1,0:T(8,128)(2,1)S(1)}, u32[]{:S(2)}, u32[]{:S(2)}) collective-permute-start(bf16[352,128]{1,0:T(8,128)(2,1)S(1)} %get-tuple-element.6), channel_id=1, source_target_pairs={{0,8},{1,9},{2,10},{3,11},{4,12},{5,13},{6,14},{7,15},{8,0},{9,1},... | collective-permute-start | bytes 270344 | tf_op jit(solution)/shard_map/ppermute | solution.py:185
  17.7 0.5 %collective-permute-start.4 = (bf16[352,128]{1,0:T(8,128)(2,1)S(1)}, bf16[352,128]{1,0:T(8,128)(2,1)S(1)}, u32[]{:S(2)}, u32[]{:S(2)}) collective-permute-start(bf16[352,128]{1,0:T(8,128)(2,1)S(1)} %get-tuple-element.6), channel_id=1, source_target_pairs={{0,24},{1,25},{2,26},{3,27},{4,28},{5,29},{6,30},{7,31},{8,16},{9,... | collective-permute-start | bytes 270344 | tf_op jit(solution)/shard_map/ppermute | solution.py:185
  18.2 0.0 copy-done.4
  18.2 0.0 collective-permute-start.5
  18.2 1.9 %collective-permute-done.3 = bf16[352,128]{1,0:T(8,128)(2,1)S(1)} collective-permute-done((bf16[352,128]{1,0:T(8,128)(2,1)S(1)}, bf16[352,128]{1,0:T(8,128)(2,1)S(1)}, u32[]{:S(2)}, u32[]{:S(2)}) %collective-permute-start.3) | collective-permute-done | bytes 90144 | tf_op jit(solution)/shard_map/ppermute | solution.py:185
  20.0 0.7 %collective-permute-done.2 = bf16[352,128]{1,0:T(8,128)(2,1)S(1)} collective-permute-done((bf16[352,128]{1,0:T(8,128)(2,1)S(1)}, bf16[352,128]{1,0:T(8,128)(2,1)S(1)}, u32[]{:S(2)}, u32[]{:S(2)}) %collective-permute-start.2) | collective-permute-done | bytes 90144 | tf_op jit(solution)/shard_map/ppermute | solution.py:185
  20.7 2.4 %collective-permute-done.4 = bf16[352,128]{1,0:T(8,128)(2,1)S(1)} collective-permute-done((bf16[352,128]{1,0:T(8,128)(2,1)S(1)}, bf16[352,128]{1,0:T(8,128)(2,1)S(1)}, u32[]{:S(2)}, u32[]{:S(2)}) %collective-permute-start.4) | collective-permute-done | bytes 90144 | tf_op jit(solution)/shard_map/ppermute | solution.py:185
  23.2 0.0 copy-start
  23.2 0.1 collective-permute-start.9
  23.2 0.0 collective-permute-done.5
  23.3 2.3 %collective-permute-start.8 = (bf16[160,128]{1,0:T(8,128)(2,1)S(1)}, bf16[160,128]{1,0:T(8,128)(2,1)S(1)}, u32[]{:S(2)}, u32[]{:S(2)}) collective-permute-start(bf16[160,128]{1,0:T(8,128)(2,1)S(1)} %collective-permute-done.5), channel_id=1, source_target_pairs={{0,24},{1,25},{2,26},{3,27},{4,28},{5,29},{6,30},{7,31},{8,16},{9,... | collective-permute-start | bytes 122888 | tf_op jit(solution)/shard_map/ppermute | solution.py:185
  25.5 0.5 %collective-permute-start.7 = (bf16[160,128]{1,0:T(8,128)(2,1)S(1)}, bf16[160,128]{1,0:T(8,128)(2,1)S(1)}, u32[]{:S(2)}, u32[]{:S(2)}) collective-permute-start(bf16[160,128]{1,0:T(8,128)(2,1)S(1)} %collective-permute-done.5), channel_id=1, source_target_pairs={{0,16},{1,17},{2,18},{3,19},{4,20},{5,21},{6,22},{7,23},{8,24},{9,... | collective-permute-start | bytes 122888 | tf_op jit(solution)/shard_map/ppermute | solution.py:185
  26.0 0.8 %collective-permute-start.6 = (bf16[160,128]{1,0:T(8,128)(2,1)S(1)}, bf16[160,128]{1,0:T(8,128)(2,1)S(1)}, u32[]{:S(2)}, u32[]{:S(2)}) collective-permute-start(bf16[160,128]{1,0:T(8,128)(2,1)S(1)} %collective-permute-done.5), channel_id=1, source_target_pairs={{0,8},{1,9},{2,10},{3,11},{4,12},{5,13},{6,14},{7,15},{8,0},{9,1},... | collective-permute-start | bytes 122888 | tf_op jit(solution)/shard_map/ppermute | solution.py:185
  26.8 1.4 %collective-permute-done.8 = bf16[160,128]{1,0:T(8,128)(2,1)S(1)} collective-permute-done((bf16[160,128]{1,0:T(8,128)(2,1)S(1)}, bf16[160,128]{1,0:T(8,128)(2,1)S(1)}, u32[]{:S(2)}, u32[]{:S(2)}) %collective-permute-start.8) | collective-permute-done | bytes 40992 | tf_op jit(solution)/shard_map/ppermute | solution.py:185
  28.2 1.3 %collective-permute-done.7 = bf16[160,128]{1,0:T(8,128)(2,1)S(1)} collective-permute-done((bf16[160,128]{1,0:T(8,128)(2,1)S(1)}, bf16[160,128]{1,0:T(8,128)(2,1)S(1)}, u32[]{:S(2)}, u32[]{:S(2)}) %collective-permute-start.7) | collective-permute-done | bytes 40992 | tf_op jit(solution)/shard_map/ppermute | solution.py:185
  29.5 0.5 %collective-permute-done.6 = bf16[160,128]{1,0:T(8,128)(2,1)S(1)} collective-permute-done((bf16[160,128]{1,0:T(8,128)(2,1)S(1)}, bf16[160,128]{1,0:T(8,128)(2,1)S(1)}, u32[]{:S(2)}, u32[]{:S(2)}) %collective-permute-start.6) | collective-permute-done | bytes 40992 | tf_op jit(solution)/shard_map/ppermute | solution.py:185
  30.0 0.0 copy-start.1
  30.1 0.1 collective-permute-start.10
  30.1 1.4 %collective-permute-done.10.refs_3_ = bf16[4,160,128]{2,1,0:T(8,128)(2,1)S(1)} collective-permute-done((bf16[4,160,128]{2,1,0:T(8,128)(2,1)S(1)}, bf16[4,160,128]{2,1,0:T(8,128)(2,1)S(1)}, u32[]{:S(2)}, u32[]{:S(2)}) %collective-permute-start.10) | collective-permute-done | bytes 163872 | tf_op jit(solution)/shard_map/ppermute | solution.py:185
  31.5 0.0 copy-start.3
  31.5 0.0 collective-permute-done.9.refs_2_
  31.5 0.0 copy-done
  31.5 0.0 copy-done.1
  31.5 0.7 %copy-done.3 = bf16[4,160,128]{2,1,0:T(8,128)(2,1)} copy-done((bf16[4,160,128]{2,1,0:T(8,128)(2,1)}, bf16[4,160,128]{2,1,0:T(8,128)(2,1)S(1)}, u32[]{:S(2)}) %copy-start.3) | copy-done | bytes 163864
  32.2 0.0 copy-start.2
  32.2 0.7 %copy-done.2 = bf16[4,352,128]{2,1,0:T(8,128)(2,1)} copy-done((bf16[4,352,128]{2,1,0:T(8,128)(2,1)}, bf16[4,352,128]{2,1,0:T(8,128)(2,1)S(1)}, u32[]{:S(2)}) %copy-start.2) | copy-done | bytes 360472
  32.9 3.4 %slab.1 = f32[2,64]{1,0:T(2,128)} custom-call(s32[4]{0:T(128)} %rows_ref.3, bf16[1,256,512]{2,1,0:T(8,128)(2,1)} %wave_ref.3, bf16[2,4,256,256]{3,2,1,0:T(8,128)(2,1)} %ops_ref.1, bf16[4,352,128]{2,1,0:T(8,128)(2,1)} %copy-done, bf16[4,160,128]{2,1,0:T(8,128)(2,1)} %copy-done.1, bf16[4,352,128]{2,1,0:T(8,128)(2,1)} %copy-done.2, bf16[4,160,128]{2,1,0:T(8,128)(2,1)} %copy-done.3), custom_call_target="tpu_custom_call" | custom-call | tf_op jit(solution)/shard_map/slab/pallas_call | solution.py:160
  (3 shorter events, 0.1 us)
Async XLA Ops:
  3.4 7.1 %collective-permute-start.1 = (bf16[160,128]{1,0:T(8,128)(2,1)}, bf16[160,128]{1,0:T(8,128)(2,1)S(1)}, u32[]{:S(2)}, u32[]{:S(2)}) collective-permute-start(bf16[160,128]{1,0:T(8,128)(2,1)} %cut.1), channel_id=1, source_target_pairs={{0,3},{1,0},{2,1},{3,2},{4,7},{5,4},{6,5},{7,6},{8,11},{9,8},{10,9... | collective-permute-start | bytes 122888 | tf_op jit(solution)/shard_map/ppermute | solution.py:185
  8.6 6.0 %collective-permute-start = (bf16[160,128]{1,0:T(8,128)(2,1)}, bf16[160,128]{1,0:T(8,128)(2,1)S(1)}, u32[]{:S(2)}, u32[]{:S(2)}) collective-permute-start(bf16[160,128]{1,0:T(8,128)(2,1)} %cut.1), channel_id=1, source_target_pairs={{0,1},{1,2},{2,3},{3,0},{4,5},{5,6},{6,7},{7,4},{8,9},{9,10},{10,1... | collective-permute-start | bytes 122888 | tf_op jit(solution)/shard_map/ppermute | solution.py:185
  9.3 8.8 %copy-start.4 = (bf16[160,128]{1,0:T(8,128)(2,1)S(1)}, bf16[160,128]{1,0:T(8,128)(2,1)}, u32[]{:S(2)}) copy-start(bf16[160,128]{1,0:T(8,128)(2,1)} %cut.1) | copy-start | bytes 122884
  14.6 5.4 %collective-permute-start.3 = (bf16[352,128]{1,0:T(8,128)(2,1)S(1)}, bf16[352,128]{1,0:T(8,128)(2,1)S(1)}, u32[]{:S(2)}, u32[]{:S(2)}) collective-permute-start(bf16[352,128]{1,0:T(8,128)(2,1)S(1)} %get-tuple-element.6), channel_id=1, source_target_pairs={{0,16},{1,17},{2,18},{3,19},{4,20},{5,21},{6,22},{7,23},{8,24},{9,... | collective-permute-start | bytes 270344 | tf_op jit(solution)/shard_map/ppermute | solution.py:185
  16.2 4.5 %collective-permute-start.2 = (bf16[352,128]{1,0:T(8,128)(2,1)S(1)}, bf16[352,128]{1,0:T(8,128)(2,1)S(1)}, u32[]{:S(2)}, u32[]{:S(2)}) collective-permute-start(bf16[352,128]{1,0:T(8,128)(2,1)S(1)} %get-tuple-element.6), channel_id=1, source_target_pairs={{0,8},{1,9},{2,10},{3,11},{4,12},{5,13},{6,14},{7,15},{8,0},{9,1},... | collective-permute-start | bytes 270344 | tf_op jit(solution)/shard_map/ppermute | solution.py:185
  17.7 5.4 %collective-permute-start.4 = (bf16[352,128]{1,0:T(8,128)(2,1)S(1)}, bf16[352,128]{1,0:T(8,128)(2,1)S(1)}, u32[]{:S(2)}, u32[]{:S(2)}) collective-permute-start(bf16[352,128]{1,0:T(8,128)(2,1)S(1)} %get-tuple-element.6), channel_id=1, source_target_pairs={{0,24},{1,25},{2,26},{3,27},{4,28},{5,29},{6,30},{7,31},{8,16},{9,... | collective-permute-start | bytes 270344 | tf_op jit(solution)/shard_map/ppermute | solution.py:185
  18.2 5.1 %collective-permute-start.5 = (bf16[160,128]{1,0:T(8,128)(2,1)S(1)}, bf16[160,128]{1,0:T(8,128)(2,1)S(1)}, u32[]{:S(2)}, u32[]{:S(2)}) collective-permute-start(bf16[160,128]{1,0:T(8,128)(2,1)S(1)} %copy-done.4), channel_id=1, source_target_pairs={{0,2},{1,3},{2,0},{3,1},{4,6},{5,7},{6,4},{7,5},{8,10},{9,11},{10,... | collective-permute-start | bytes 122888 | tf_op jit(solution)/shard_map/ppermute | solution.py:185
  23.2 8.4 %copy-start = (bf16[4,352,128]{2,1,0:T(8,128)(2,1)}, bf16[4,352,128]{2,1,0:T(8,128)(2,1)S(1)}, u32[]{:S(2)}) copy-start(bf16[4,352,128]{2,1,0:T(8,128)(2,1)S(1)} %pad_maximum_fusion.refs_0_) | copy-start | bytes 1081348
  23.2 8.4 %collective-permute-start.9 = (bf16[4,352,128]{2,1,0:T(8,128)(2,1)S(1)}, bf16[4,352,128]{2,1,0:T(8,128)(2,1)S(1)}, u32[]{:S(2)}, u32[]{:S(2)}) collective-permute-start(bf16[4,352,128]{2,1,0:T(8,128)(2,1)S(1)} %pad_maximum_fusion.refs_0_), channel_id=1, source_target_pairs={{0,4},{1,5},{2,6},{3,7},{4,0},{5,1},{6,2},{7,3},{8,12},{9,13},{10,... | collective-permute-start | bytes 1081352 | tf_op jit(solution)/shard_map/ppermute | solution.py:185
  23.3 5.0 %collective-permute-start.8 = (bf16[160,128]{1,0:T(8,128)(2,1)S(1)}, bf16[160,128]{1,0:T(8,128)(2,1)S(1)}, u32[]{:S(2)}, u32[]{:S(2)}) collective-permute-start(bf16[160,128]{1,0:T(8,128)(2,1)S(1)} %collective-permute-done.5), channel_id=1, source_target_pairs={{0,24},{1,25},{2,26},{3,27},{4,28},{5,29},{6,30},{7,31},{8,16},{9,... | collective-permute-start | bytes 122888 | tf_op jit(solution)/shard_map/ppermute | solution.py:185
  25.5 4.0 %collective-permute-start.7 = (bf16[160,128]{1,0:T(8,128)(2,1)S(1)}, bf16[160,128]{1,0:T(8,128)(2,1)S(1)}, u32[]{:S(2)}, u32[]{:S(2)}) collective-permute-start(bf16[160,128]{1,0:T(8,128)(2,1)S(1)} %collective-permute-done.5), channel_id=1, source_target_pairs={{0,16},{1,17},{2,18},{3,19},{4,20},{5,21},{6,22},{7,23},{8,24},{9,... | collective-permute-start | bytes 122888 | tf_op jit(solution)/shard_map/ppermute | solution.py:185
  26.0 4.0 %collective-permute-start.6 = (bf16[160,128]{1,0:T(8,128)(2,1)S(1)}, bf16[160,128]{1,0:T(8,128)(2,1)S(1)}, u32[]{:S(2)}, u32[]{:S(2)}) collective-permute-start(bf16[160,128]{1,0:T(8,128)(2,1)S(1)} %collective-permute-done.5), channel_id=1, source_target_pairs={{0,8},{1,9},{2,10},{3,11},{4,12},{5,13},{6,14},{7,15},{8,0},{9,1},... | collective-permute-start | bytes 122888 | tf_op jit(solution)/shard_map/ppermute | solution.py:185
  30.0 1.5 %copy-start.1 = (bf16[4,160,128]{2,1,0:T(8,128)(2,1)}, bf16[4,160,128]{2,1,0:T(8,128)(2,1)S(1)}, u32[]{:S(2)}) copy-start(bf16[4,160,128]{2,1,0:T(8,128)(2,1)S(1)} %pad_maximum_fusion.1.refs_1_) | copy-start | bytes 491524
  30.1 1.5 %collective-permute-start.10 = (bf16[4,160,128]{2,1,0:T(8,128)(2,1)S(1)}, bf16[4,160,128]{2,1,0:T(8,128)(2,1)S(1)}, u32[]{:S(2)}, u32[]{:S(2)}) collective-permute-start(bf16[4,160,128]{2,1,0:T(8,128)(2,1)S(1)} %pad_maximum_fusion.1.refs_1_), channel_id=1, source_target_pairs={{0,4},{1,5},{2,6},{3,7},{4,0},{5,1},{6,2},{7,3},{8,12},{9,13},{10,... | collective-permute-start | bytes 491528 | tf_op jit(solution)/shard_map/ppermute | solution.py:185
  31.5 0.7 %copy-start.3 = (bf16[4,160,128]{2,1,0:T(8,128)(2,1)}, bf16[4,160,128]{2,1,0:T(8,128)(2,1)S(1)}, u32[]{:S(2)}) copy-start(bf16[4,160,128]{2,1,0:T(8,128)(2,1)S(1)} %collective-permute-done.10.refs_3_) | copy-start | bytes 491524
  32.2 0.7 %copy-start.2 = (bf16[4,352,128]{2,1,0:T(8,128)(2,1)}, bf16[4,352,128]{2,1,0:T(8,128)(2,1)S(1)}, u32[]{:S(2)}) copy-start(bf16[4,352,128]{2,1,0:T(8,128)(2,1)S(1)} %collective-permute-done.9.refs_2_) | copy-start | bytes 1081348
